TPU v7x, 32 devices: a whole 2x2x4 slice. The times are simulated.
32 devices in a mesh: parts: 2 (over y), pair: 4 (over x, core), sub: 4 (over z).
Axes of the slice: x: 2, y: 2, z: 4, core: 2. Of those that a mesh axis runs over, the one named last changes fastest.
Arguments:
- features: bfloat16 [64, 1024, 256], P(('parts', 'pair'), 'sub'), parts along dimension 0, may hold values from -7 to 7
- counts: int32 [64], P('parts'), parts along dimension 0, may hold values from 256 to 1024
- pair_table: int32 [8, 4, 2], P('parts'), parts along dimension 0, may hold values from -1 to 31, as said below
- w_qk: bfloat16 [256, 256], replicated, may hold values from -0.75 to 0.75
- w_value: bfloat16 [256, 256], replicated, may hold values from -0.375 to 0.375
- w_out: bfloat16 [256, 256], replicated, may hold values from -1.5 to 1.5
- w_merge_in: bfloat16 [512, 512], replicated, may hold values from -0.25 to 0.25
- w_merge_out: bfloat16 [512, 256], replicated, may hold values from -0.25 to 0.25
Outputs:
- updated: bfloat16 [64, 1024, 256], P(('parts', 'pair'), 'sub'), parts along dimension 0
There are 2 independent parts, one for each index of `parts`. A program takes and returns all parts, laid end to end along the dimension named above; an argument that names none is the same for every part. Nothing has to cross between parts.
Inputs may be any that keep to these rules, and one draw needn't show every extreme that they name: `pair_table`: row g lists the pairs owned by index g of pair, one slot per index of sub; -1 in both entries marks an empty slot. A live slot names two images of different groups, image i belonging to group i // 8. Over the live slots of one owner, at most 2 named images (counted with repetition) belong to any one group; some owner has all 4 slots live and reaches that bound for every group.
All inputs are finite; a program needn't handle non-finite values.
Results may differ from a plain program's by a relative error of at most 0.0067.
Values may be sent and summed in bfloat16 or wider, within the bound.
A program may use at most 64 MiB of HBM per device.

v0:
```python
import jax
import jax.numpy as jnp
from jax import lax
from jax.sharding import PartitionSpec as P

HEADS = 4
ln_eps = 1e-05


def layer_norm(hidden):
    center = jnp.mean(hidden, axis=-1, keepdims=True)
    centered = hidden - center
    variance = jnp.mean(centered * centered, axis=-1, keepdims=True)
    return centered * lax.rsqrt(variance + ln_eps)


def pair_messages(left_feats, right_feats, left_count, right_count, w_qk, w_value, head_count):
    points = left_feats.shape[0]
    model_width = left_feats.shape[1]
    head_dim = model_width // head_count
    stacked = jnp.concatenate([left_feats, right_feats], axis=0)
    query_key = jnp.dot(stacked, w_qk, preferred_element_type=jnp.float32).astype(jnp.bfloat16)
    values = jnp.dot(stacked, w_value, preferred_element_type=jnp.float32).astype(jnp.bfloat16)
    row_ids = lax.broadcasted_iota(jnp.int32, (points, 1), 0)
    col_ids = lax.broadcasted_iota(jnp.int32, (1, points), 1)
    col_valid = col_ids < right_count
    row_valid = row_ids < left_count
    score_scale = head_dim ** (-0.5)
    to_left = []
    to_right = []
    for head_index in range(head_count):
        head_lo = head_index * head_dim
        q_left = query_key[:points, head_lo : head_lo + head_dim]
        q_right = query_key[points:, head_lo : head_lo + head_dim]
        v_left = values[:points, head_lo : head_lo + head_dim]
        v_right = values[points:, head_lo : head_lo + head_dim]
        scores = (
            lax.dot_general(
                q_left, q_right, (((1,), (1,)), ((), ())), preferred_element_type=jnp.float32
            )
            * score_scale
        )
        masked = jnp.where(col_valid, scores, -jnp.inf)
        row_top = jnp.max(masked, axis=1, keepdims=True)
        row_exp = jnp.exp(masked - row_top)
        row_total = jnp.sum(row_exp, axis=1, keepdims=True)
        to_left.append(
            jnp.dot(row_exp.astype(jnp.bfloat16), v_right, preferred_element_type=jnp.float32)
            / row_total
        )
        col_masked = jnp.where(row_valid, scores, -jnp.inf)
        col_top = jnp.max(col_masked, axis=0, keepdims=True)
        col_exp = jnp.exp(col_masked - col_top)
        col_total = jnp.sum(col_exp, axis=0, keepdims=True)
        summed = lax.dot_general(
            col_exp.astype(jnp.bfloat16),
            v_left,
            (((0,), (0,)), ((), ())),
            preferred_element_type=jnp.float32,
        )
        to_right.append(summed / col_total.reshape(points, 1))
    return (
        jnp.concatenate(to_left, axis=1).astype(jnp.bfloat16),
        jnp.concatenate(to_right, axis=1).astype(jnp.bfloat16),
    )


def local(features, counts, pair_table, w_qk, w_value, w_out, w_merge_in, w_merge_out):
    n_pair = lax.axis_size("pair")
    n_sub = lax.axis_size("sub")
    me_group = lax.axis_index("pair")
    me_sub = lax.axis_index("sub")
    img_grp, kp_block, model_width = features.shape
    per_src = 2 * n_sub // n_pair
    positions = 2 * n_sub
    slot_table = pair_table.reshape(n_pair, positions)
    slot_live = slot_table >= 0
    source = jnp.where(slot_live, slot_table // img_grp, -1)
    group_ids = jnp.arange(n_pair, dtype=jnp.int32)
    src_hot = (source[:, :, None] == group_ids[None, None, :]).astype(jnp.int32)
    src_rank = jnp.sum((jnp.cumsum(src_hot, axis=1) - 1) * src_hot, axis=2)
    src_rank = jnp.where(slot_live, src_rank, -1)
    slot_ids = jnp.arange(per_src, dtype=jnp.int32)
    from_me = source == me_group
    send_match = from_me[:, None, :] & (src_rank[:, None, :] == slot_ids[None, :, None])
    send_local = jnp.sum(
        jnp.where(send_match, slot_table[:, None, :] - me_group * img_grp, 0), axis=2
    )
    send_ok = jnp.any(send_match, axis=2)
    my_table = lax.dynamic_index_in_dim(slot_table, me_group, 0, keepdims=False)
    my_live = lax.dynamic_index_in_dim(slot_live, me_group, 0, keepdims=False)
    my_source = lax.dynamic_index_in_dim(source, me_group, 0, keepdims=False)
    my_rank = lax.dynamic_index_in_dim(src_rank, me_group, 0, keepdims=False)
    outgoing = jnp.take(features, send_local.reshape(-1), axis=0).reshape(
        n_pair, per_src, kp_block, model_width
    )
    outgoing = jnp.where(send_ok[:, :, None, None], outgoing, jnp.zeros_like(outgoing))
    arrived = lax.all_to_all(outgoing, "pair", split_axis=0, concat_axis=0, tiled=True)
    flat_index = jnp.maximum(my_source * per_src + my_rank, 0)
    picked = jnp.take(arrived.reshape(n_pair * per_src, kp_block, model_width), flat_index, axis=0)
    picked = jnp.where(my_live[:, None, None], picked, jnp.zeros_like(picked))
    grouped = picked.reshape(n_sub, 2, kp_block, model_width)
    pair_rows = lax.all_to_all(grouped, "sub", split_axis=0, concat_axis=2, tiled=True)
    slot_pair = jnp.maximum(lax.dynamic_slice_in_dim(my_table, 2 * me_sub, 2), 0)
    pair_counts = jnp.take(counts, slot_pair)
    to_left, to_right = pair_messages(
        pair_rows[0, 0], pair_rows[0, 1], pair_counts[0], pair_counts[1], w_qk, w_value, HEADS
    )
    outbound = jnp.stack([to_left, to_right], axis=0)[None]
    returned = lax.all_to_all(outbound, "sub", split_axis=2, concat_axis=0, tiled=True)
    returned = returned.reshape(positions, kp_block, model_width)
    returned = jnp.where(my_live[:, None, None], returned, jnp.zeros_like(returned))
    position_ids = jnp.arange(positions, dtype=jnp.int32)
    inverse = (
        (my_source[None, None, :] == group_ids[:, None, None])
        & (my_rank[None, None, :] == slot_ids[None, :, None])
        & my_live[None, None, :]
    )
    inv_pos = jnp.sum(jnp.where(inverse, position_ids[None, None, :], 0), axis=2)
    inv_ok = jnp.any(inverse, axis=2)
    homeward = jnp.take(returned, inv_pos.reshape(-1), axis=0).reshape(
        n_pair, per_src, kp_block, model_width
    )
    homeward = jnp.where(inv_ok[:, :, None, None], homeward, jnp.zeros_like(homeward))
    home_msgs = lax.all_to_all(homeward, "pair", split_axis=0, concat_axis=0, tiled=True)
    local_ids = jnp.arange(img_grp, dtype=jnp.int32)
    owner_hot = ((send_local.reshape(1, -1) == local_ids[:, None]) & send_ok.reshape(1, -1)).astype(
        jnp.bfloat16
    )
    msg_total = jnp.dot(
        owner_hot,
        home_msgs.reshape(n_pair * per_src, kp_block * model_width),
        preferred_element_type=jnp.float32,
    )
    global_ids = me_group * img_grp + local_ids
    use_count = jnp.sum(
        (pair_table.reshape(1, -1) == global_ids[:, None]).astype(jnp.int32), axis=1
    )
    divisor = jnp.maximum(use_count, 1).astype(jnp.float32)
    mean_msg = (msg_total / divisor[:, None]).astype(jnp.bfloat16)
    own_rows = features.reshape(-1, model_width)
    lifted = jnp.dot(
        mean_msg.reshape(-1, model_width), w_out, preferred_element_type=jnp.float32
    ).astype(jnp.bfloat16)
    hidden = jnp.dot(own_rows, w_merge_in[:model_width], preferred_element_type=jnp.float32)
    hidden = hidden + jnp.dot(lifted, w_merge_in[model_width:], preferred_element_type=jnp.float32)
    active = jax.nn.gelu(layer_norm(hidden), approximate=False).astype(jnp.bfloat16)
    updated = own_rows.astype(jnp.float32) + jnp.dot(
        active, w_merge_out, preferred_element_type=jnp.float32
    )
    return updated.astype(jnp.bfloat16).reshape(img_grp, kp_block, model_width)


def solution(mesh):
    in_specs = (
        P(("parts", "pair"), "sub", None),
        P("parts"),
        P("parts", None, None),
        P(),
        P(),
        P(),
        P(),
        P(),
    )
    out_specs = P(("parts", "pair"), "sub", None)
    return jax.shard_map(local, mesh=mesh, in_specs=in_specs, out_specs=out_specs, check_vma=False)
```

profile of v0, /device:TPU:0, one launch (start us, length us, event | category | flops | bytes accessed | tf_op | source)
XLA Modules:
  0.0 154.1 jit_solution(910745184698559716)
XLA Ops:
  0.0 0.8 copy.48
  2.8 1.8 %gather_fusion.1 = bf16[8,256,256]{2,1,0:T(8,128)(2,1)S(1)} fusion(bf16[8,256,256]{2,1,0:T(8,128)(2,1)} %param.10, s32[1024]{0:T(1024)S(1)} %pad_clamp_fusion.2), kind=kCustom, calls=%fused_computation.clone | custom fusion | bytes 2097184 | tf_op jit(solution)/shard_map/jit(_take)/gather | solution.py:94
  4.8 1.1 broadcast_select_fusion.2
  5.9 4.4 %all-to-all-start = ((bf16[4,2,256,256]{3,2,1,0:T(8,128)(2,1)}), bf16[4,2,256,256]{3,2,1,0:T(8,128)(2,1)S(1)}, u32[]{:S(2)}, u32[]{:S(2)}) async-start(bf16[4,2,256,256]{3,2,1,0:T(8,128)(2,1)} %broadcast_select_fusion.2), calls=%async_computation | async-start | bytes 2097152 | tf_op jit(solution)/shard_map/all_to_all | solution.py:98
  10.3 14.4 %all-to-all-done = bf16[4,2,256,256]{3,2,1,0:T(8,128)(2,1)S(1)} async-done(((bf16[4,2,256,256]{3,2,1,0:T(8,128)(2,1)}), bf16[4,2,256,256]{3,2,1,0:T(8,128)(2,1)S(1)}, u32[]{:S(2)}, u32[]{:S(2)}) %all-to-all-start) | async-done | bytes 1048608 | tf_op jit(solution)/shard_map/all_to_all | solution.py:98
  25.4 1.2 select_select_fusion
  26.5 5.6 %all-to-all-start.1 = ((bf16[4,2,256,256]{3,2,1,0:T(8,128)(2,1)}), bf16[4,2,256,256]{3,2,1,0:T(8,128)(2,1)S(1)}, u32[]{:S(2)}, u32[]{:S(2)}) async-start(bf16[4,2,256,256]{3,2,1,0:T(8,128)(2,1)} %bitcast.8), calls=%async_computation.1 | async-start | bytes 2097152 | tf_op jit(solution)/shard_map/all_to_all | solution.py:103
  33.8 1.3 iota_compare_fusion.1
  35.0 22.5 %all-to-all-done.1 = bf16[4,2,256,256]{3,2,1,0:T(8,128)(2,1)S(1)} async-done(((bf16[4,2,256,256]{3,2,1,0:T(8,128)(2,1)}), bf16[4,2,256,256]{3,2,1,0:T(8,128)(2,1)S(1)}, u32[]{:S(2)}, u32[]{:S(2)}) %all-to-all-start.1) | async-done | bytes 1048608 | tf_op jit(solution)/shard_map/all_to_all | solution.py:103
  58.2 0.7 fusion.141
  59.7 0.7 fusion.133
  60.9 1.9 %select_reduce_fusion.7 = (f32[1024]{0:T(1024)S(1)}, f32[1024]{0:T(1024)S(1)}, f32[1024]{0:T(1024)S(1)}, f32[1024]{0:T(1024)S(1)}, f32[1024,1024]{1,0:T(8,128)S(1)}) fusion(pred[1024]{0:T(1024)(128)(4,1)S(1)} %get-tuple-element.47, f32[1024,1024]{1,0:T(8,128)S(1)} %fusion.141, f32[1024,1024]{1,0:T(8,128)S(1)} %fusion.137, f32[1024,1024]{1,0:T(8,128)S(1)} %fusion.133, ...), kind=kOutput, calls=%fused_computation.41 | convolution fusion | flops 146796544 | bytes 17056768 | tf_op jit(solution)/shard_map/dot_general | solution.py:38
  62.8 6.2 %fusion.17 = (f32[1024]{0:T(1024)S(1)}, f32[1024]{0:T(1024)S(1)}, f32[1024]{0:T(1024)S(1)}, f32[1024]{0:T(1024)S(1)}, f32[1024]{0:T(1024)S(1)}, /*index=5*/f32[1024]{0:T(1024)S(1)}, f32[1024]{0:T(1024)S(1)}, f32[1024]{0:T(1024)S(1)}) fusion(f32[1024,1024]{1,0:T(8,128)S(1)} %fusion.133, f32[1024]{0:T(1024)S(1)} %get-tuple-element.23, ...), kind=kLoop, calls=%fused_computation.48 | loop fusion | flops 25157632 | bytes 16828416 | tf_op jit(solution)/shard_map/reduce_sum | solution.py:46
  69.0 4.2 %fusion.19 = (f32[1024]{0:T(1024)S(1)}, f32[1024]{0:T(1024)S(1)}, f32[1024]{0:T(1024)S(1)}, f32[1024]{0:T(1024)S(1)}) fusion(f32[1024,1024]{1,0:T(8,128)S(1)} %get-tuple-element.39, f32[1024]{0:T(1024)S(1)} %get-tuple-element.14, pred[1024]{0:T(1024)(128)(4,1)S(1)} %get-tuple-element.46, f32[1024]{0:T(1024)S(1)} %get-tuple-element.16, ...), kind=kLoop, calls=%fused_computation.50 | loop fusion | flops 16773120 | bytes 16811008 | tf_op jit(solution)/shard_map/reduce_sum | solution.py:54
  73.2 1.1 fusion.95
  74.3 1.0 fusion.59
  75.4 1.1 fusion.122
  76.5 1.0 fusion.86
  77.6 1.1 fusion.113
  78.7 1.0 fusion.77
  79.8 1.0 fusion.68
  80.8 1.1 fusion.104
  82.0 2.0 %copy.61 = bf16[1,2,1024,256]{3,1,0,2:T(2,128)(2,1)} copy(bf16[1,2,1024,256]{2,3,1,0:T(8,128)(2,1)S(1)} %maximum_bitcast_fusion) | data formatting | bytes 2097152 | tf_op jit(solution)/shard_map/broadcast_in_dim | solution.py:109
  84.1 3.5 %all-to-all-start.2 = ((bf16[1,2,1024,256]{3,1,0,2:T(2,128)(2,1)}), bf16[1,2,1024,256]{3,1,0,2:T(2,128)(2,1)S(1)}, u32[]{:S(2)}, u32[]{:S(2)}) async-start(bf16[1,2,1024,256]{3,1,0,2:T(2,128)(2,1)} %copy.61), calls=%async_computation.2 | async-start | bytes 2097152 | tf_op jit(solution)/shard_map/all_to_all | solution.py:110
  88.2 24.7 %all-to-all-done.2 = bf16[1,2,1024,256]{3,1,0,2:T(2,128)(2,1)S(1)} async-done(((bf16[1,2,1024,256]{3,1,0,2:T(2,128)(2,1)}), bf16[1,2,1024,256]{3,1,0,2:T(2,128)(2,1)S(1)}, u32[]{:S(2)}, u32[]{:S(2)}) %all-to-all-start.2) | async-done | bytes 1048608 | tf_op jit(solution)/shard_map/all_to_all | solution.py:110
  114.0 1.1 broadcast_select_fusion.3
  115.1 3.7 %all-to-all-start.3 = ((bf16[4,2,256,256]{3,2,1,0:T(8,128)(2,1)}), bf16[4,2,256,256]{3,2,1,0:T(8,128)(2,1)S(1)}, u32[]{:S(2)}, u32[]{:S(2)}) async-start(bf16[4,2,256,256]{3,2,1,0:T(8,128)(2,1)} %broadcast_select_fusion.3), calls=%async_computation.3 | async-start | bytes 2097152 | tf_op jit(solution)/shard_map/all_to_all | solution.py:125
  119.1 2.7 %fusion.126 = f32[2048,512]{0,1:T(8,128)} fusion(bf16[2048,256]{1,0:T(8,128)(2,1)S(1)} %bitcast.65, bf16[512,512]{1,0:T(8,128)(2,1)S(1)} %copy-done.4), kind=kOutput, calls=%fused_computation.115 | convolution fusion | flops 536870912 | bytes 5505024 | tf_op jit(solution)/shard_map/dot_general | solution.py:145
  121.8 11.3 %all-to-all-done.3 = bf16[4,2,256,256]{3,2,1,0:T(8,128)(2,1)S(1)} async-done(((bf16[4,2,256,256]{3,2,1,0:T(8,128)(2,1)}), bf16[4,2,256,256]{3,2,1,0:T(8,128)(2,1)S(1)}, u32[]{:S(2)}, u32[]{:S(2)}) %all-to-all-start.3) | async-done | bytes 1048608 | tf_op jit(solution)/shard_map/all_to_all | solution.py:125
  134.6 5.3 %fusion.214 = (f32[2048]{0:T(1024)S(1)}, f32[2048,512]{0,1:T(8,128)}) fusion(f32[2048,512]{0,1:T(8,128)} %fusion.126, bf16[512,512]{1,0:T(8,128)(2,1)} %param.16, bf16[2048,256]{1,0:T(8,128)(2,1)S(1)} %reshape.377, bf16[256,256]{1,0:T(8,128)(2,1)S(1)} %copy-done.5), kind=kOutput, calls=%fused_computation.240 | convolution fusion | flops 807925760 | bytes 9838592 | tf_op jit(solution)/shard_map/dot_general | solution.py:146
  139.9 2.8 %multiply_reduce_fusion = f32[2048]{0:T(1024)S(1)} fusion(f32[2048,512]{0,1:T(8,128)} %get-tuple-element.41, f32[2048]{0:T(1024)S(1)} %broadcast_multiply_fusion), kind=kLoop, calls=%fused_computation.23 | loop fusion | flops 3143680 | bytes 4210688 | tf_op jit(solution)/shard_map/reduce_sum | solution.py:13
  143.4 10.8 %fusion.27 = bf16[2048,256]{1,0:T(8,128)(2,1)} fusion(bf16[512,256]{1,0:T(8,128)(2,1)S(1)} %copy-done, bf16[2048,256]{1,0:T(8,128)(2,1)S(1)} %bitcast.66, f32[2048,512]{0,1:T(8,128)S(1)} %copy-done.2, f32[2048]{0:T(1024)S(1)} %add_rsqrt_fusion, f32[2048]{0:T(1024)S(1)} %broadcast_multiply_fusion), kind=kOutput, calls=%fused_computation.60 | convolution fusion | flops 608698368 | bytes 6569984 | tf_op jit(solution)/shard_map/dot_general | solution.py:148
  (75 shorter events, 10.3 us)
Async XLA Ops:
  0.0 142.7 %copy-start = (bf16[512,256]{1,0:T(8,128)(2,1)S(1)}, bf16[512,256]{1,0:T(8,128)(2,1)}, u32[]{:S(2)}) copy-start(bf16[512,256]{1,0:T(8,128)(2,1)} %param.17) | copy-start | bytes 786436
  5.9 26.4 %copy-start.1 = (s32[32]{0:T(128)S(1)}, s32[32]{0:T(128)}, u32[]{:S(2)}) copy-start(s32[32]{0:T(128)} %param.11) | copy-start | bytes 388
  5.9 18.8 %all-to-all-start = ((bf16[4,2,256,256]{3,2,1,0:T(8,128)(2,1)}), bf16[4,2,256,256]{3,2,1,0:T(8,128)(2,1)S(1)}, u32[]{:S(2)}, u32[]{:S(2)}) async-start(bf16[4,2,256,256]{3,2,1,0:T(8,128)(2,1)} %broadcast_select_fusion.2), calls=%async_computation | async-start | bytes 2097152 | tf_op jit(solution)/shard_map/all_to_all | solution.py:98
  25.4 32.4 %copy-start.7 = (bf16[256,256]{1,0:T(8,128)(2,1)S(1)}, bf16[256,256]{1,0:T(8,128)(2,1)}, u32[]{:S(2)}) copy-start(bf16[256,256]{1,0:T(8,128)(2,1)} %param.13) | copy-start | bytes 393220
  26.5 31.0 %all-to-all-start.1 = ((bf16[4,2,256,256]{3,2,1,0:T(8,128)(2,1)}), bf16[4,2,256,256]{3,2,1,0:T(8,128)(2,1)S(1)}, u32[]{:S(2)}, u32[]{:S(2)}) async-start(bf16[4,2,256,256]{3,2,1,0:T(8,128)(2,1)} %bitcast.8), calls=%async_computation.1 | async-start | bytes 2097152 | tf_op jit(solution)/shard_map/all_to_all | solution.py:103
  58.9 1.5 copy-start.8
  82.0 5.7 %copy-start.6 = (s32[4,4,2]{1,2,0:T(2,128)S(1)}, s32[4,4,2]{1,2,0:T(2,128)}, u32[]{:S(2)}) copy-start(s32[4,4,2]{1,2,0:T(2,128)} %param.12) | copy-start | bytes 388
  84.1 28.8 %all-to-all-start.2 = ((bf16[1,2,1024,256]{3,1,0,2:T(2,128)(2,1)}), bf16[1,2,1024,256]{3,1,0,2:T(2,128)(2,1)S(1)}, u32[]{:S(2)}, u32[]{:S(2)}) async-start(bf16[1,2,1024,256]{3,1,0,2:T(2,128)(2,1)} %copy.61), calls=%async_computation.2 | async-start | bytes 2097152 | tf_op jit(solution)/shard_map/all_to_all | solution.py:110
  113.2 5.9 %copy-start.3 = (bf16[8,256,256]{2,1,0:T(8,128)(2,1)S(1)}, bf16[8,256,256]{2,1,0:T(8,128)(2,1)}, u32[]{:S(2)}) copy-start(bf16[8,256,256]{2,1,0:T(8,128)(2,1)} %param.10) | copy-start | bytes 3145732
  113.9 5.3 %copy-start.4 = (bf16[512,512]{1,0:T(8,128)(2,1)S(1)}, bf16[512,512]{1,0:T(8,128)(2,1)}, u32[]{:S(2)}) copy-start(bf16[512,512]{1,0:T(8,128)(2,1)} %param.16) | copy-start | bytes 1572868
  115.1 17.9 %all-to-all-start.3 = ((bf16[4,2,256,256]{3,2,1,0:T(8,128)(2,1)}), bf16[4,2,256,256]{3,2,1,0:T(8,128)(2,1)S(1)}, u32[]{:S(2)}, u32[]{:S(2)}) async-start(bf16[4,2,256,256]{3,2,1,0:T(8,128)(2,1)} %broadcast_select_fusion.3), calls=%async_computation.3 | async-start | bytes 2097152 | tf_op jit(solution)/shard_map/all_to_all | solution.py:125
  133.7 0.9 copy-start.5
  139.9 3.4 %copy-start.2 = (f32[2048,512]{0,1:T(8,128)S(1)}, f32[2048,512]{0,1:T(8,128)}, u32[]{:S(2)}) copy-start(f32[2048,512]{0,1:T(8,128)} %get-tuple-element.41) | copy-start | bytes 12582916
where the time goes:
time: 155 us; the launch traced here: 154 us
  waiting for transfers between devices  72.9 us (47%)
  matrix products  33 us (21%)
  other arithmetic  20.4 us (13%)
  starting transfers between devices  17.2 us (11%)
  local copies, waits for them, and re-layouts  10.3 us (7%)
    all_to_all x1, waiting for transfers between devices, local(): lax.all_to_all(outbound, 'sub', split_axis=2, concat_axis=0, tiled=True)  24.7 us
    all_to_all x1, waiting for transfers between devices, local(): lax.all_to_all(grouped, 'sub', split_axis=0, concat_axis=2, tiled=True)  22.5 us
    all_to_all x1, waiting for transfers between devices, local(): lax.all_to_all(outgoing, 'pair', split_axis=0, concat_axis=0, tiled=True)  14.4 us
    all_to_all x1, waiting for transfers between devices, local(): lax.all_to_all(homeward, 'pair', split_axis=0, concat_axis=0, tiled=True)  11.3 us
    dot_general x1, matrix products, local(): jnp.dot(active, w_merge_out, preferred_element_type=jnp.float32)  10.8 us
    reduce_sum x1, other arithmetic, pair_messages(): row_total = jnp.sum(row_exp, axis=1, keepdims=True)  6.18 us
    all_to_all x1, starting transfers between devices, local(): lax.all_to_all(grouped, 'sub', split_axis=0, concat_axis=2, tiled=True)  5.6 us
    dot_general x1, matrix products, local(): jnp.dot(lifted, w_merge_in[model_width:], preferred_element_type=jnp.floa...  5.34 us
  transfers between devices with their start and end apart: 4, of which 4 were waited for; matrix products, arithmetic and copies ran while one was open for 4% of the time, Pallas kernels for 0%

commit v1 on v0

--- a/solution.py
+++ b/solution.py
@@ -107,7 +107,15 @@
         pair_rows[0, 0], pair_rows[0, 1], pair_counts[0], pair_counts[1], w_qk, w_value, HEADS
     )
     outbound = jnp.stack([to_left, to_right], axis=0)[None]
-    returned = lax.all_to_all(outbound, "sub", split_axis=2, concat_axis=0, tiled=True)
+    returned = jnp.concatenate(
+        lax.all_to_all(
+            jnp.stack(jnp.split(outbound, lax.axis_size("sub"), axis=2)),
+            axis_name="sub",
+            split_axis=0,
+            concat_axis=0,
+        ),
+        axis=0,
+    )
     returned = returned.reshape(positions, kp_block, model_width)
     returned = jnp.where(my_live[:, None, None], returned, jnp.zeros_like(returned))
     position_ids = jnp.arange(positions, dtype=jnp.int32)

time: 155 us -> 154 us (level)
  local copies, waits for them, and re-layouts: 10.3 us -> 8.64 us
    broadcast_in_dim x1 -> x0, local copies, waits for them, and re-layouts: 2.04 us -> none  [local(): outbound = jnp.stack([to_left, to_right], axis=0)[None]]
where the time goes in v1:
time: 154 us
  waiting for transfers between devices  72.9 us (47%)
  matrix products  33 us (21%)
  other arithmetic  21.5 us (14%)
  starting transfers between devices  17.2 us (11%)
  local copies, waits for them, and re-layouts  8.64 us (6%)
    all_to_all x1, waiting for transfers between devices, local(): lax.all_to_all(jnp.stack(jnp.split(outbound, lax.axis_size('sub'), axis=2...  24.7 us
    all_to_all x1, waiting for transfers between devices, local(): lax.all_to_all(grouped, 'sub', split_axis=0, concat_axis=2, tiled=True)  22.5 us
    all_to_all x1, waiting for transfers between devices, local(): lax.all_to_all(outgoing, 'pair', split_axis=0, concat_axis=0, tiled=True)  14.4 us
    all_to_all x1, waiting for transfers between devices, local(): lax.all_to_all(homeward, 'pair', split_axis=0, concat_axis=0, tiled=True)  11.3 us
    dot_general x1, matrix products, local(): jnp.dot(active, w_merge_out, preferred_element_type=jnp.float32)  10.8 us
    reduce_sum x1, other arithmetic, pair_messages(): row_total = jnp.sum(row_exp, axis=1, keepdims=True)  6.18 us
    all_to_all x1, starting transfers between devices, local(): lax.all_to_all(grouped, 'sub', split_axis=0, concat_axis=2, tiled=True)  5.6 us
    dot_general x1, matrix products, local(): jnp.dot(lifted, w_merge_in[model_width:], preferred_element_type=jnp.floa...  5.34 us
  transfers between devices with their start and end apart: 4, of which 4 were waited for; matrix products, arithmetic and copies ran while one was open for 4% of the time, Pallas kernels for 0%

profile of v1, /device:TPU:0, one launch (start us, length us, event | category | flops | bytes accessed | tf_op | source)
XLA Modules:
  0.0 153.6 jit_solution(7211658153560071123)
XLA Ops:
  0.0 0.8 copy.32
  2.8 1.8 %gather_fusion.1 = bf16[8,256,256]{2,1,0:T(8,128)(2,1)S(1)} fusion(bf16[8,256,256]{2,1,0:T(8,128)(2,1)} %param.10, s32[1024]{0:T(1024)S(1)} %pad_clamp_fusion.2), kind=kCustom, calls=%fused_computation.clone | custom fusion | bytes 2097184 | tf_op jit(solution)/shard_map/jit(_take)/gather | solution.py:94
  4.8 1.1 broadcast_select_fusion.3
  5.9 4.4 %all-to-all-start = ((bf16[4,2,256,256]{3,2,1,0:T(8,128)(2,1)}), bf16[4,2,256,256]{3,2,1,0:T(8,128)(2,1)S(1)}, u32[]{:S(2)}, u32[]{:S(2)}) async-start(bf16[4,2,256,256]{3,2,1,0:T(8,128)(2,1)} %broadcast_select_fusion.3), calls=%async_computation | async-start | bytes 2097152 | tf_op jit(solution)/shard_map/all_to_all | solution.py:98
  10.3 14.4 %all-to-all-done = bf16[4,2,256,256]{3,2,1,0:T(8,128)(2,1)S(1)} async-done(((bf16[4,2,256,256]{3,2,1,0:T(8,128)(2,1)}), bf16[4,2,256,256]{3,2,1,0:T(8,128)(2,1)S(1)}, u32[]{:S(2)}, u32[]{:S(2)}) %all-to-all-start) | async-done | bytes 1048608 | tf_op jit(solution)/shard_map/all_to_all | solution.py:98
  25.4 1.2 select_select_fusion
  26.5 5.6 %all-to-all-start.1 = ((bf16[4,2,256,256]{3,2,1,0:T(8,128)(2,1)}), bf16[4,2,256,256]{3,2,1,0:T(8,128)(2,1)S(1)}, u32[]{:S(2)}, u32[]{:S(2)}) async-start(bf16[4,2,256,256]{3,2,1,0:T(8,128)(2,1)} %bitcast.8), calls=%async_computation.1 | async-start | bytes 2097152 | tf_op jit(solution)/shard_map/all_to_all | solution.py:103
  33.8 1.3 iota_compare_fusion.1
  35.0 22.5 %all-to-all-done.1 = bf16[4,2,256,256]{3,2,1,0:T(8,128)(2,1)S(1)} async-done(((bf16[4,2,256,256]{3,2,1,0:T(8,128)(2,1)}), bf16[4,2,256,256]{3,2,1,0:T(8,128)(2,1)S(1)}, u32[]{:S(2)}, u32[]{:S(2)}) %all-to-all-start.1) | async-done | bytes 1048608 | tf_op jit(solution)/shard_map/all_to_all | solution.py:103
  58.2 0.7 fusion.141
  59.7 0.7 fusion.133
  60.9 1.9 %select_reduce_fusion.7 = (f32[1024]{0:T(1024)S(1)}, f32[1024]{0:T(1024)S(1)}, f32[1024]{0:T(1024)S(1)}, f32[1024]{0:T(1024)S(1)}, f32[1024,1024]{1,0:T(8,128)S(1)}) fusion(pred[1024]{0:T(1024)(128)(4,1)S(1)} %get-tuple-element.49, f32[1024,1024]{1,0:T(8,128)S(1)} %fusion.141, f32[1024,1024]{1,0:T(8,128)S(1)} %fusion.137, f32[1024,1024]{1,0:T(8,128)S(1)} %fusion.133, ...), kind=kOutput, calls=%fused_computation.41 | convolution fusion | flops 146796544 | bytes 17056768 | tf_op jit(solution)/shard_map/dot_general | solution.py:38
  62.8 6.2 %fusion.17 = (f32[1024]{0:T(1024)S(1)}, f32[1024]{0:T(1024)S(1)}, f32[1024]{0:T(1024)S(1)}, f32[1024]{0:T(1024)S(1)}, f32[1024]{0:T(1024)S(1)}, /*index=5*/f32[1024]{0:T(1024)S(1)}, f32[1024]{0:T(1024)S(1)}, f32[1024]{0:T(1024)S(1)}) fusion(f32[1024,1024]{1,0:T(8,128)S(1)} %fusion.133, f32[1024]{0:T(1024)S(1)} %get-tuple-element.23, ...), kind=kLoop, calls=%fused_computation.48 | loop fusion | flops 25157632 | bytes 16828416 | tf_op jit(solution)/shard_map/reduce_sum | solution.py:46
  69.0 4.2 %fusion.19 = (f32[1024]{0:T(1024)S(1)}, f32[1024]{0:T(1024)S(1)}, f32[1024]{0:T(1024)S(1)}, f32[1024]{0:T(1024)S(1)}) fusion(f32[1024,1024]{1,0:T(8,128)S(1)} %get-tuple-element.43, f32[1024]{0:T(1024)S(1)} %get-tuple-element.14, pred[1024]{0:T(1024)(128)(4,1)S(1)} %get-tuple-element.48, f32[1024]{0:T(1024)S(1)} %get-tuple-element.16, ...), kind=kLoop, calls=%fused_computation.50 | loop fusion | flops 16773120 | bytes 16811008 | tf_op jit(solution)/shard_map/reduce_sum | solution.py:54
  73.2 1.1 fusion.95
  74.3 1.0 fusion.59
  75.4 1.1 fusion.122
  76.5 1.0 fusion.86
  77.6 1.1 fusion.113
  78.7 1.0 fusion.77
  79.8 1.0 fusion.68
  80.8 1.1 fusion.104
  82.1 1.1 pad_maximum_fusion.1
  83.2 3.5 %all-to-all-start.2 = ((bf16[4,1,2,256,256]{3,4,2,1,0:T(8,128)(2,1)}), bf16[4,1,2,256,256]{3,4,2,1,0:T(8,128)(2,1)S(1)}, u32[]{:S(2)}, u32[]{:S(2)}) async-start(bf16[4,1,2,256,256]{3,4,2,1,0:T(8,128)(2,1)} %pad_maximum_fusion.1), calls=%async_computation.2 | async-start | bytes 2097152 | tf_op jit(solution)/shard_map/all_to_all | solution.py:111
  87.3 24.7 %all-to-all-done.2 = bf16[4,1,2,256,256]{3,4,2,1,0:T(8,128)(2,1)S(1)} async-done(((bf16[4,1,2,256,256]{3,4,2,1,0:T(8,128)(2,1)}), bf16[4,1,2,256,256]{3,4,2,1,0:T(8,128)(2,1)S(1)}, u32[]{:S(2)}, u32[]{:S(2)}) %all-to-all-start.2) | async-done | bytes 1048608 | tf_op jit(solution)/shard_map/all_to_all | solution.py:111
  113.5 1.1 broadcast_select_fusion.4
  114.6 3.7 %all-to-all-start.3 = ((bf16[4,2,256,256]{3,2,1,0:T(8,128)(2,1)}), bf16[4,2,256,256]{3,2,1,0:T(8,128)(2,1)S(1)}, u32[]{:S(2)}, u32[]{:S(2)}) async-start(bf16[4,2,256,256]{3,2,1,0:T(8,128)(2,1)} %broadcast_select_fusion.4), calls=%async_computation.3 | async-start | bytes 2097152 | tf_op jit(solution)/shard_map/all_to_all | solution.py:133
  118.6 2.7 %fusion.126 = f32[2048,512]{0,1:T(8,128)} fusion(bf16[2048,256]{1,0:T(8,128)(2,1)S(1)} %bitcast.69, bf16[512,512]{1,0:T(8,128)(2,1)S(1)} %copy-done.4), kind=kOutput, calls=%fused_computation.120 | convolution fusion | flops 536870912 | bytes 5505024 | tf_op jit(solution)/shard_map/dot_general | solution.py:153
  121.2 11.3 %all-to-all-done.3 = bf16[4,2,256,256]{3,2,1,0:T(8,128)(2,1)S(1)} async-done(((bf16[4,2,256,256]{3,2,1,0:T(8,128)(2,1)}), bf16[4,2,256,256]{3,2,1,0:T(8,128)(2,1)S(1)}, u32[]{:S(2)}, u32[]{:S(2)}) %all-to-all-start.3) | async-done | bytes 1048608 | tf_op jit(solution)/shard_map/all_to_all | solution.py:133
  134.0 5.3 %fusion.214 = (f32[2048]{0:T(1024)S(1)}, f32[2048,512]{0,1:T(8,128)}) fusion(f32[2048,512]{0,1:T(8,128)} %fusion.126, bf16[512,512]{1,0:T(8,128)(2,1)} %param.16, bf16[2048,256]{1,0:T(8,128)(2,1)S(1)} %reshape.372, bf16[256,256]{1,0:T(8,128)(2,1)S(1)} %copy-done.5), kind=kOutput, calls=%fused_computation.245 | convolution fusion | flops 807925760 | bytes 9838592 | tf_op jit(solution)/shard_map/dot_general | solution.py:154
  139.4 2.8 %multiply_reduce_fusion = f32[2048]{0:T(1024)S(1)} fusion(f32[2048,512]{0,1:T(8,128)} %get-tuple-element.45, f32[2048]{0:T(1024)S(1)} %broadcast_multiply_fusion), kind=kLoop, calls=%fused_computation.23 | loop fusion | flops 3143680 | bytes 4210688 | tf_op jit(solution)/shard_map/reduce_sum | solution.py:13
  142.8 10.8 %fusion.27 = bf16[2048,256]{1,0:T(8,128)(2,1)} fusion(bf16[512,256]{1,0:T(8,128)(2,1)S(1)} %copy-done, bf16[2048,256]{1,0:T(8,128)(2,1)S(1)} %bitcast.70, f32[2048,512]{0,1:T(8,128)S(1)} %copy-done.2, f32[2048]{0:T(1024)S(1)} %add_rsqrt_fusion, f32[2048]{0:T(1024)S(1)} %broadcast_multiply_fusion), kind=kOutput, calls=%fused_computation.60 | convolution fusion | flops 608698368 | bytes 6569984 | tf_op jit(solution)/shard_map/dot_general | solution.py:156
  (76 shorter events, 10.7 us)
Async XLA Ops:
  0.0 142.2 %copy-start = (bf16[512,256]{1,0:T(8,128)(2,1)S(1)}, bf16[512,256]{1,0:T(8,128)(2,1)}, u32[]{:S(2)}) copy-start(bf16[512,256]{1,0:T(8,128)(2,1)} %param.17) | copy-start | bytes 786436
  5.9 26.4 %copy-start.1 = (s32[32]{0:T(128)S(1)}, s32[32]{0:T(128)}, u32[]{:S(2)}) copy-start(s32[32]{0:T(128)} %param.11) | copy-start | bytes 388
  5.9 18.8 %all-to-all-start = ((bf16[4,2,256,256]{3,2,1,0:T(8,128)(2,1)}), bf16[4,2,256,256]{3,2,1,0:T(8,128)(2,1)S(1)}, u32[]{:S(2)}, u32[]{:S(2)}) async-start(bf16[4,2,256,256]{3,2,1,0:T(8,128)(2,1)} %broadcast_select_fusion.3), calls=%async_computation | async-start | bytes 2097152 | tf_op jit(solution)/shard_map/all_to_all | solution.py:98
  25.4 32.4 %copy-start.7 = (bf16[256,256]{1,0:T(8,128)(2,1)S(1)}, bf16[256,256]{1,0:T(8,128)(2,1)}, u32[]{:S(2)}) copy-start(bf16[256,256]{1,0:T(8,128)(2,1)} %param.13) | copy-start | bytes 393220
  26.5 31.0 %all-to-all-start.1 = ((bf16[4,2,256,256]{3,2,1,0:T(8,128)(2,1)}), bf16[4,2,256,256]{3,2,1,0:T(8,128)(2,1)S(1)}, u32[]{:S(2)}, u32[]{:S(2)}) async-start(bf16[4,2,256,256]{3,2,1,0:T(8,128)(2,1)} %bitcast.8), calls=%async_computation.1 | async-start | bytes 2097152 | tf_op jit(solution)/shard_map/all_to_all | solution.py:103
  58.9 1.5 copy-start.8
  82.0 4.9 %copy-start.6 = (s32[4,4,2]{1,2,0:T(2,128)S(1)}, s32[4,4,2]{1,2,0:T(2,128)}, u32[]{:S(2)}) copy-start(s32[4,4,2]{1,2,0:T(2,128)} %param.12) | copy-start | bytes 388
  83.2 28.8 %all-to-all-start.2 = ((bf16[4,1,2,256,256]{3,4,2,1,0:T(8,128)(2,1)}), bf16[4,1,2,256,256]{3,4,2,1,0:T(8,128)(2,1)S(1)}, u32[]{:S(2)}, u32[]{:S(2)}) async-start(bf16[4,1,2,256,256]{3,4,2,1,0:T(8,128)(2,1)} %pad_maximum_fusion.1), calls=%async_computation.2 | async-start | bytes 2097152 | tf_op jit(solution)/shard_map/all_to_all | solution.py:111
  112.7 5.9 %copy-start.3 = (bf16[8,256,256]{2,1,0:T(8,128)(2,1)S(1)}, bf16[8,256,256]{2,1,0:T(8,128)(2,1)}, u32[]{:S(2)}) copy-start(bf16[8,256,256]{2,1,0:T(8,128)(2,1)} %param.10) | copy-start | bytes 3145732
  113.3 5.3 %copy-start.4 = (bf16[512,512]{1,0:T(8,128)(2,1)S(1)}, bf16[512,512]{1,0:T(8,128)(2,1)}, u32[]{:S(2)}) copy-start(bf16[512,512]{1,0:T(8,128)(2,1)} %param.16) | copy-start | bytes 1572868
  114.6 17.9 %all-to-all-start.3 = ((bf16[4,2,256,256]{3,2,1,0:T(8,128)(2,1)}), bf16[4,2,256,256]{3,2,1,0:T(8,128)(2,1)S(1)}, u32[]{:S(2)}, u32[]{:S(2)}) async-start(bf16[4,2,256,256]{3,2,1,0:T(8,128)(2,1)} %broadcast_select_fusion.4), calls=%async_computation.3 | async-start | bytes 2097152 | tf_op jit(solution)/shard_map/all_to_all | solution.py:133
  133.1 0.9 copy-start.5
  139.4 3.4 %copy-start.2 = (f32[2048,512]{0,1:T(8,128)S(1)}, f32[2048,512]{0,1:T(8,128)}, u32[]{:S(2)}) copy-start(f32[2048,512]{0,1:T(8,128)} %get-tuple-element.45) | copy-start | bytes 12582916
